TPU v7x, 512 devices: a whole 4x8x8 slice. The times are simulated.
512 devices in a mesh: tile: 64 (over y, z_lo, core), img: 8 (over z_hi, x).
Axes of the slice: x: 4, y: 8, z: 8 (z_hi: 2, z_lo: 4; z = z_hi * 4 + z_lo), core: 2. Of those that a mesh axis runs over, the one named last changes fastest.
Arguments:
- heights: float32 [64, 64, 128], P('tile'), may hold values from -1.5 to 1.5
- albedo: float32 [64, 64, 128], P('tile'), may hold values from 0.5 to 1.5
- blocks: bfloat16 [64, 8, 64, 64, 128], P('tile', 'img'), may hold values from 0 to 1
- block_params: bfloat16 [64, 8, 64, 8], P('tile', 'img'), may hold values from -1 to 2, as said below
- block_dest: int32 [64, 8, 64, 1], P('tile', 'img'), may hold values from 0 to 63; in each aligned block of 64 rows (0 to 63, 64 to 127, ..., all dimensions but the last counted through in order) at most 2 rows name the same one
Outputs:
- grad_heights: float32 [64, 64, 128], P('tile', 'img')
- grad_albedo: float32 [64, 64, 128], P('tile', 'img')
Inputs may be any that keep to these rules, and one draw needn't show every extreme that they name: `block_params`: columns 0 to 2 are a unit sun vector whose third entry lies between 0.05 and 0.43, columns 3 to 5 a unit view vector whose first two entries lie within -0.15 and 0.15, column 6 lies between 0.2 and 0.9 and column 7 between 0.5 and 2. `block_dest`: of the blocks held by one device, at most 2 lie on any one tile, and in every draw some device holds exactly 2 blocks of some tile.
All inputs are finite; a program needn't handle non-finite values.
Results may differ from a plain program's by a relative error of at most 0.0003.
Values may be sent and summed in bfloat16 or wider, within the bound.
No kernel may reach another device: no remote copies, remote signals or barrier semaphores. Data moves between devices by JAX's collectives and lax.ppermute only.
A program may use at most 64 MiB of HBM per device.

v0:
```python
import jax
import jax.numpy as jnp
from jax import lax
from jax.experimental import pallas as pl
from jax.experimental.pallas import tpu as pltpu
from jax.sharding import Mesh
from jax.sharding import PartitionSpec as P


SMOOTH = 0.0025
PARAMS = 8
STRIP = 16
ROWS, CLASSES, CORES, HALVES, DEPTH = 8, 4, 2, 2, 4
RING = CLASSES * HALVES
TILE = ("y", "zl", "c")
IMG = ("zh", "x")

SMEM = pl.BlockSpec(memory_space=pltpu.SMEM)
VMEM = pl.BlockSpec(memory_space=pltpu.VMEM)


def ring_shift(value, steps):
    pairs = []
    for low in range(CLASSES):
        for core in range(CORES):
            for high in range(HALVES):
                z = (high * CLASSES + low + steps * (1 - 2 * core)) % RING
                source = (low * CORES + core) * HALVES + high
                pairs.append((source, ((z % CLASSES) * CORES + core) * HALVES + z // CLASSES))
    return lax.ppermute(value, ("zl", "c", "zh"), pairs)


def column_shift(value, steps):
    count = CLASSES * CORES
    pairs = [(k, k + steps) for k in range(count) if 0 <= k + steps < count]
    return lax.ppermute(value, ("zl", "c"), pairs)


def in_vmem(*arrays):
    return [pltpu.with_memory_space_constraint(a, pltpu.VMEM) for a in arrays]


def fill_table(dest_ref, table):
    number = dest_ref.shape[0]

    def clear(index, carry):
        table[index] = number
        return carry

    lax.fori_loop(0, table.shape[0], clear, 0, unroll=8)

    def note(index, carry):
        place = dest_ref[index] * 2
        second = (table[place] < number).astype(jnp.int32)
        table[place + second] = index
        return carry

    lax.fori_loop(0, number, note, 0, unroll=4)


def first_turn(core):
    return 1 + core * (CLASSES - 2)


def pack_kernel(
    here_ref, dest_ref, params_ref, blocks_hbm, near_ref, first_ref, second_ref, far_ref, other_ref,
    blocks_ref, sem, table, shifted, columns, rim, lines,
):
    number, tile_rows, tile_cols = blocks_hbm.shape
    fetch = pltpu.make_async_copy(blocks_hbm, blocks_ref.at[:number], sem)
    fetch.start()
    blocks_ref[number] = jnp.zeros((tile_rows, tile_cols), jnp.bfloat16)
    for part in range(3):
        shifted[part, number:, :] = jnp.zeros((8, tile_cols), jnp.float32)
    for part in range(2):
        rim[part, number // 2 :, :] = jnp.zeros((8, tile_cols), jnp.float32)
    fill_table(dest_ref, table)
    upright = params_ref[...].astype(jnp.float32)
    upright = jnp.concatenate([upright, jnp.zeros((PARAMS, tile_cols - number), jnp.float32)], axis=1)
    plain = turned(upright)[:number]
    for k in range(3):
        shifted[k, :number, :] = plain if k == 0 else pltpu.roll(plain, k * PARAMS, 1)

    fetch.wait()

    lane8 = lax.broadcasted_iota(jnp.int32, (8, tile_cols), 1)
    sub8 = lax.broadcasted_iota(jnp.int32, (8, tile_cols), 0)
    pick = jnp.where(((sub8 == 0) & (lane8 == tile_cols - 1)) | ((sub8 == 1) & (lane8 == 0)), 1.0, 0.0).astype(jnp.bfloat16)
    flat = lax.dot_general(
        pick,
        blocks_ref[:number].reshape(number * tile_rows, tile_cols),
        (((1,), (1,)), ((), ())),
        preferred_element_type=jnp.float32,
    )
    pairs = number // 2
    for m in range(pairs):
        part = slice(m * tile_cols, (m + 1) * tile_cols)
        columns[0, m : m + 1, :] = flat[0:1, part]
        columns[1, m : m + 1, :] = flat[1:2, part]
    left_half = lax.broadcasted_iota(jnp.int32, (pairs, tile_cols), 1) < tile_rows
    last, first = columns[0], columns[1]
    rim[0, :pairs, :] = jnp.where(left_half, last, pltpu.roll(first, tile_rows, 1))
    rim[1, :pairs, :] = jnp.where(left_half, pltpu.roll(last, tile_rows, 1), first)

    low, core = here_ref[0], here_ref[1]
    count = CLASSES * CORES
    west_half = lax.broadcasted_iota(jnp.int32, (1, tile_cols), 1) < tile_rows
    pixels = ROWS * tile_rows
    turn = first_turn(core)
    mine = [
        (0, near_ref.at[0], near_ref.at[1]),
        (turn, first_ref.at[0], first_ref.at[1]),
        (CLASSES // 2, far_ref.at[0], far_ref.at[1]),
        (CLASSES - turn, second_ref.at[0], second_ref.at[1]),
    ]

    for kind in range(CORES):
        for d in range(CLASSES):
            step, *units = (d, other_ref.at[d, 0], other_ref.at[d, 1]) if kind else mine[d]
            column = ((low + step) % CLASSES) * CORES + (core + kind) % CORES

            def place(step, carry):
                found = []
                for row in (step * 2, step * 2 + 1):
                    tile = row * count + column
                    for slot in (0, 1):
                        block = table[2 * tile + slot]
                        west = jnp.where(column > 0, table[jnp.maximum(2 * tile - 2, 0) + slot], number)
                        east = jnp.where(
                            column < count - 1, table[jnp.minimum(2 * tile + 2, 2 * ROWS * count - 2) + slot], number
                        )
                        line = shifted[0, pl.ds(block, 1), :] + shifted[1, pl.ds(west, 1), :] + shifted[2, pl.ds(east, 1), :]
                        sides = [rim[index % 2, pl.ds(index // 2, 1), :] for index in (west, east)]
                        found.append((row, slot, blocks_ref[block], jnp.where(west_half, sides[0], sides[1]), line))
                for row, slot, values, side, line in found:
                    start = pl.multiple_of(row * tile_rows, tile_rows)
                    units[slot][pl.ds(start, tile_rows), :] = values
                    lines[0, slot, pl.ds(row, 1), :] = side
                    lines[1, slot, pl.ds(row, 1), :] = line
                return carry

            lax.fori_loop(0, ROWS // 2, place, 0)
            for slot in (0, 1):
                for k in (0, 1):
                    units[slot][pixels + k * ROWS : pixels + (k + 1) * ROWS, :] = lines[k, slot].astype(jnp.bfloat16)


def pack(here, dest, params, blocks):
    number, tile_rows, tile_cols = blocks.shape
    unit = (ROWS * tile_rows + 2 * ROWS, tile_cols)
    return pl.pallas_call(
        pack_kernel,
        out_shape=[pltpu.VMEM(lead + unit, jnp.bfloat16) for lead in ((2,), (2,), (2,), (2,), (CLASSES, 2))],
        in_specs=[SMEM, SMEM, VMEM, pl.BlockSpec(memory_space=pltpu.HBM)],
        out_specs=[VMEM] * 5,
        scratch_shapes=[
            pltpu.VMEM((number + 1, tile_rows, tile_cols), jnp.bfloat16),
            pltpu.SemaphoreType.DMA,
            pltpu.SMEM((2 * ROWS * CLASSES * CORES,), jnp.int32),
            pltpu.VMEM((3, number + 8, tile_cols), jnp.float32),
            pltpu.VMEM((2, number // 2, tile_cols), jnp.float32),
            pltpu.VMEM((2, number // 2 + 8, tile_cols), jnp.float32),
            pltpu.VMEM((2, 2, ROWS, tile_cols), jnp.float32),
        ],
        cost_estimate=pl.CostEstimate(flops=0, bytes_accessed=6 << 20, transcendentals=0),
        compiler_params=pltpu.CompilerParams(vmem_limit_bytes=8 << 20),
        name="pack",
    )(here, *[pltpu.with_memory_space_constraint(a, pltpu.HBM) for a in (dest, params, blocks)])


def join_kernel(here_ref, swapped_ref, first_own, second_own, far_own, first_ref, second_ref, far_ref):
    core = here_ref[1]
    turn = first_turn(core)
    first_ref[0:2] = first_own[...]
    first_ref[2:4] = swapped_ref[turn]
    second_ref[0:2] = second_own[...]
    second_ref[2:4] = swapped_ref[CLASSES - turn]
    far_ref[0:2] = far_own[...]
    far_ref[2:4] = swapped_ref[CLASSES // 2]


def join(here, swapped, *own):
    unit = swapped.shape[2:]
    return pl.pallas_call(
        join_kernel,
        out_shape=[pltpu.VMEM((n,) + unit, swapped.dtype) for n in (4, 4, 4)],
        in_specs=[SMEM] + [VMEM] * 4,
        out_specs=[VMEM] * 3,
        cost_estimate=pl.CostEstimate(flops=0, bytes_accessed=2 << 20, transcendentals=0),
        compiler_params=pltpu.CompilerParams(vmem_limit_bytes=4 << 20),
        name="join",
    )(here, *in_vmem(swapped, *own))


def copies_kernel(height_ref, albedo_ref, rows_ref, out_ref):
    tile_rows = height_ref.shape[0]
    for row in range(ROWS):
        out_ref[row, :tile_rows, :] = height_ref[...]
        out_ref[row, tile_rows : 2 * tile_rows, :] = albedo_ref[...]
        out_ref[row, 2 * tile_rows :, :] = rows_ref[...]


def make_copies(height, albedo, rows):
    return pl.pallas_call(
        copies_kernel,
        out_shape=pltpu.VMEM((ROWS, 2 * height.shape[0] + ROWS, height.shape[1]), jnp.float32),
        in_specs=[VMEM] * 3,
        out_specs=VMEM,
        cost_estimate=pl.CostEstimate(flops=0, bytes_accessed=1 << 20, transcendentals=0),
        compiler_params=pltpu.CompilerParams(vmem_limit_bytes=4 << 20),
        name="copies",
    )(*in_vmem(height, albedo, rows))


def turned(rows):
    size = rows.shape[1]
    return jnp.transpose(jnp.concatenate([rows, jnp.zeros((size - rows.shape[0], size), rows.dtype)]))


def maps_kernel(column_ref, got_ref, maps_ref, tall, side):
    tile_cols = got_ref.shape[2]
    tile_rows = (got_ref.shape[1] - ROWS) // 2
    pixels = ROWS * tile_rows
    column = column_ref[0]
    lane = lax.broadcasted_iota(jnp.int32, (tile_rows, tile_cols), 1)

    def finish(part, p, q, albedo):
        maps_ref[0, part, :] = p
        maps_ref[1, part, :] = q
        maps_ref[2, part, :] = 1.0 / jnp.sqrt(1.0 + p * p + q * q)
        maps_ref[3, part, :] = albedo

    for row in range(ROWS):
        tall[8 + row * tile_rows : 8 + (row + 1) * tile_rows, :] = got_ref[row, :tile_rows, :]
    tall[7:8, :] = got_ref[0, 0:1, :]
    tall[8 + pixels : 9 + pixels, :] = got_ref[ROWS - 1, tile_rows - 1 : tile_rows, :]
    beside, beyond, shade, mine = [
        jnp.concatenate([got_ref[row, 2 * tile_rows + k : 2 * tile_rows + k + 1, :] for row in range(ROWS)]) for k in range(4)
    ]
    side[...] = turned(beside)
    for row in range(ROWS):
        start = 8 + row * tile_rows
        height = tall[start : start + tile_rows, :]
        west = pltpu.roll(side[:tile_rows, :], (tile_cols - row) % tile_cols, 1)
        east = pltpu.roll(side[tile_rows:, :], tile_cols - 1 - row, 1)
        before = jnp.where(lane == 0, jnp.where(column == 0, height, west), pltpu.roll(height, 1, 1))
        after = jnp.where(
            lane == tile_cols - 1,
            jnp.where(column == CLASSES * CORES - 1, height, east),
            pltpu.roll(height, tile_cols - 1, 1),
        )
        p = (after - before) * 0.5
        q = (tall[start + 1 : start + 1 + tile_rows, :] - tall[start - 1 : start - 1 + tile_rows, :]) * 0.5
        finish(slice(row * tile_rows, (row + 1) * tile_rows), p, q, got_ref[row, tile_rows : 2 * tile_rows, :])

    lane = lax.broadcasted_iota(jnp.int32, (ROWS, tile_cols), 1)
    p = jnp.where(lane < tile_rows, mine - beyond, beyond - mine) * 0.5
    lower = jnp.concatenate([pltpu.roll(beside, tile_rows - 1, 1)[1:], beside[ROWS - 1 :]])
    upper = jnp.concatenate([beside[:1], pltpu.roll(beside, tile_cols - tile_rows + 1, 1)[:-1]])
    place = lane % tile_rows
    following = jnp.where(place == tile_rows - 1, lower, pltpu.roll(beside, tile_cols - 1, 1))
    preceding = jnp.where(place == 0, upper, pltpu.roll(beside, 1, 1))
    finish(slice(pixels, pixels + ROWS), p, (following - preceding) * 0.5, shade)


def make_maps(column, got):
    tile_cols = got.shape[2]
    pixels = ROWS * (got.shape[1] - ROWS) // 2
    return pl.pallas_call(
        maps_kernel,
        out_shape=pltpu.VMEM((4, pixels + ROWS, tile_cols), jnp.float32),
        in_specs=[SMEM, VMEM],
        out_specs=VMEM,
        scratch_shapes=[
            pltpu.VMEM((pixels + 16, tile_cols), jnp.float32),
            pltpu.VMEM((tile_cols, tile_cols), jnp.float32),
        ],
        cost_estimate=pl.CostEstimate(flops=0, bytes_accessed=3 << 20, transcendentals=0),
        compiler_params=pltpu.CompilerParams(vmem_limit_bytes=4 << 20),
        name="maps",
    )(column, *in_vmem(got))


def add_block(maps, totals, values, bright):
    pw, qw, w, albedo = maps
    sum_x, sum_y, sum_z, shade = totals
    sx, sy, sz, vx, vy, vz, mix, gain = values
    mix2, rest = mix * 2.0, (1.0 - mix) * 0.5
    vx, vy, vz = vx * 2.0, vy * 2.0, vz * 2.0
    ci = sz * w - sx * pw - sy * qw
    ce = vz * w - vx * pw - vy * qw
    square = ci * ci + SMOOTH
    inv_root = lax.rsqrt(square)
    mu = ci + square * inv_root
    inv = 1.0 / (mu + ce)
    k = mix2 * inv
    shading = mu * (k + rest)
    weight = gain * albedo
    gs = weight * (weight * shading - bright.astype(jnp.float32))
    shade = shade + gs * shading
    gi = (gs * (k * (ce * inv) + rest)) * (mu * inv_root)
    ge = (gs * k) * (mu * inv)
    return (
        sum_x + (gi * sx - ge * vx),
        sum_y + (gi * sy - ge * vy),
        sum_z + (gi * sz - ge * vz),
        shade,
    )


def terms_kernel(scale, with_sums, picks, *refs):
    column_ref, maps_ref, *refs = refs
    sums_ref = None
    if with_sums:
        sums_ref, *refs = refs
    got, refs = refs[: len(picks)], refs[len(picks) :]
    out_ref, lines, params, sem, *refs = refs
    units = [ref.at[pick] for ref, some in zip(got, picks) for pick in some]
    tile_cols = maps_ref.shape[2]
    pixels = maps_ref.shape[1] - ROWS
    tile_rows = pixels // ROWS
    for index, unit in enumerate(units):
        lines[index * ROWS : (index + 1) * ROWS, :] = unit[pixels + ROWS :, :].astype(jnp.float32)
    copy = pltpu.make_async_copy(lines, params, sem)
    copy.start()
    copy.wait()

    def run(part, size, values_of):
        p, q, w, albedo = (maps_ref[k, part, :] for k in range(4))
        if with_sums:
            totals = tuple(sums_ref[k, part, :] for k in range(4))
        else:
            totals = (jnp.zeros((size, tile_cols), jnp.float32),) * 4
        maps = (p * w, q * w, w, albedo)
        for number, unit in enumerate(units):
            totals = add_block(maps, totals, values_of(number), unit[part, :])
        if scale is None:
            for k, total in enumerate(totals):
                out_ref[k, part, :] = total
            return None
        sum_x, sum_y, sum_z, shade = totals
        up = (w * w * w) * (sum_z - p * sum_x - q * sum_y)
        half_x = (-(w * sum_x) - p * up) * (0.5 * scale)
        half_y = (-(w * sum_y) - q * up) * (0.5 * scale)
        return half_x, half_y, shade * scale / albedo

    def strip(index, carry):
        first = pl.multiple_of(index * STRIP, STRIP)
        row = index // (tile_rows // STRIP)
        result = run(pl.ds(first, STRIP), STRIP, lambda number: [params[number * ROWS + row, k] for k in range(PARAMS)])
        if result is not None:
            slope_x, slope_y, _ = refs
            slope_x[pl.ds(first, STRIP), :] = result[0]
            slope_y[pl.ds(pl.multiple_of(first + 8, 8), STRIP), :] = result[1]
            for half in range(STRIP // 8):
                out_ref[index * (STRIP // 8) + half, 8:16, :] = result[2][half * 8 : half * 8 + 8]
        return carry

    lax.fori_loop(0, pixels // STRIP, strip, 0)

    west_half = lax.broadcasted_iota(jnp.int32, (ROWS, tile_cols), 1) < tile_rows

    def side_values(number):
        rows = lines[number * ROWS : (number + 1) * ROWS, :]
        values = []
        for k in range(PARAMS):
            west, east = (
                jnp.broadcast_to(rows[:, n * PARAMS + k : n * PARAMS + k + 1], (ROWS, tile_cols)) for n in (1, 2)
            )
            values.append(jnp.where(west_half, west, east))
        return values

    result = run(slice(pixels, pixels + ROWS), ROWS, side_values)
    if result is None:
        return

    slope_x, slope_y, side = refs
    column = column_ref[0]
    side[...] = turned(result[0])
    slope_y[7:8, :] = -slope_y[8:9, :]
    slope_y[8 + pixels : 9 + pixels, :] = -slope_y[7 + pixels : 8 + pixels, :]
    lane = lax.broadcasted_iota(jnp.int32, (tile_rows, tile_cols), 1)
    for row in range(ROWS):
        start = row * tile_rows
        here = slope_x[start : start + tile_rows, :]
        west = pltpu.roll(side[:tile_rows, :], (tile_cols - row) % tile_cols, 1)
        east = pltpu.roll(side[tile_rows:, :], tile_cols - 1 - row, 1)
        before = jnp.where(lane == 0, jnp.where(column == 0, -here, west), pltpu.roll(here, 1, 1))
        after = jnp.where(
            lane == tile_cols - 1,
            jnp.where(column == CLASSES * CORES - 1, -here, east),
            pltpu.roll(here, tile_cols - 1, 1),
        )
        spread = before - after + slope_y[start + 7 : start + 7 + tile_rows, :] - slope_y[start + 9 : start + 9 + tile_rows, :]
        for group in range(tile_rows // 8):
            out_ref[row * (tile_rows // 8) + group, 0:8, :] = spread[group * 8 : group * 8 + 8]


def terms(column, maps, sums, got, scale):
    arrays, picks = zip(*got)
    count = sum(len(some) for some in picks)
    given = [maps] + ([] if sums is None else [sums]) + list(arrays)
    rows, cols = maps.shape[1:]
    scratch = [
        pltpu.VMEM((count * ROWS, cols), jnp.float32),
        pltpu.SMEM((count * ROWS, cols), jnp.float32),
        pltpu.SemaphoreType.DMA,
    ]
    if scale is None:
        out = (4, rows, cols)
    else:
        out = ((rows - ROWS) // 8, 16, cols)
        scratch += [pltpu.VMEM((rows - ROWS, cols), jnp.float32), pltpu.VMEM((rows - ROWS + 16, cols), jnp.float32)]
        scratch += [pltpu.VMEM((cols, cols), jnp.float32)]
    return pl.pallas_call(
        lambda *refs: terms_kernel(scale, sums is not None, picks, *refs),
        out_shape=pltpu.VMEM(out, jnp.float32),
        in_specs=[SMEM] + [VMEM] * len(given),
        out_specs=VMEM,
        scratch_shapes=scratch,
        cost_estimate=pl.CostEstimate(flops=60 * count * rows * cols, bytes_accessed=4 << 20, transcendentals=0),
        compiler_params=pltpu.CompilerParams(vmem_limit_bytes=4 << 20),
    )(column, *in_vmem(*given))


EACH2 = [(0,), (1,)]
EACH4 = EACH2 + [(2,), (3,)]


def body(heights, albedo, blocks, block_params, block_dest):
    column_here = lax.axis_index(("zl", "c"))
    tile_rows, tile_cols = heights.shape[1:]
    block_count = block_dest.shape[2]

    height, shade = heights[0], albedo[0]
    first, last = jnp.stack([height[:, 0], height[:, 1], shade[:, 0]]), jnp.stack([height[:, -1], height[:, -2], shade[:, -1]])
    from_west = column_shift(last, 1)
    from_east = column_shift(first, -1)

    here = jnp.stack([lax.axis_index("zl"), lax.axis_index("c")]).astype(jnp.int32)
    near, *own, other = pack(
        here,
        block_dest.reshape(block_count),
        block_params.reshape(block_count, PARAMS).T,
        blocks.reshape(block_count, tile_rows, tile_cols),
    )
    swapped = lax.ppermute(other, "c", [(0, 1), (1, 0)])
    to_first, to_second, to_far = join(here, swapped, *own)
    far = ring_shift(to_far, 2)
    next0 = ring_shift(to_first, 1)
    next1 = ring_shift(to_second, -1)

    beside = jnp.concatenate([from_west, from_east], axis=1)
    mine = jnp.concatenate([first[:1], last[:1]], axis=1)
    rows = jnp.concatenate([beside, mine, jnp.zeros((ROWS - 4, tile_cols), jnp.float32)])
    copies = make_copies(height, shade, rows)
    gathered = lax.all_to_all(copies, "y", split_axis=0, concat_axis=0, tiled=True)
    column = column_here.reshape(1).astype(jnp.int32)
    maps = make_maps(column, gathered)

    sums = terms(column, maps, None, [(near, [(0,), (1,)]), (swapped, [(0, 0), (0, 1)])], None)
    sums = terms(column, maps, sums, [(far, EACH4)], None)
    sums = terms(column, maps, sums, [(next0, EACH4)], None)
    parts = terms(column, maps, sums, [(next1, EACH4)], 1.0 / block_count)
    summed = jnp.sum(lax.all_to_all(parts, ("y",) + IMG, split_axis=0, concat_axis=0, tiled=True), axis=0)
    half = tile_rows // (HALVES * DEPTH)
    return (summed[None, :half], summed[None, half:])


def solution(mesh):
    physical = Mesh(mesh.devices.reshape(ROWS, CLASSES, CORES, HALVES, DEPTH), TILE + IMG)
    placed = (
        P(TILE, None, None),
        P(TILE, None, None),
        P(TILE, IMG, None, None, None),
        P(TILE, IMG, None, None),
        P(TILE, IMG, None, None),
    )

    return jax.shard_map(
        body,
        mesh=physical,
        in_specs=placed,
        out_specs=(P(TILE, IMG, None), P(TILE, IMG, None)),
        check_vma=False,
    )
```

profile of v0, /device:TPU:6, one launch (start us, length us, event | category | flops | bytes accessed | tf_op | source)
XLA Modules:
  0.0 102.7 jit_solution(10435434322210158810)
XLA Ops:
  0.6 0.0 copy-start.1
  0.6 0.0 copy-start
  0.7 0.1 pad_add_fusion.here_ref
  0.7 5.7 %pack.1 = (bf16[2,528,128]{2,1,0:T(8,128)(2,1)S(1)}, bf16[2,528,128]{2,1,0:T(8,128)(2,1)S(1)}, bf16[2,528,128]{2,1,0:T(8,128)(2,1)S(1)}, bf16[2,528,128]{2,1,0:T(8,128)(2,1)S(1)}, bf16[4,2,528,128]{3,2,1,0:T(8,128)(2,1)}) custom-call(s32[2]{0:T(128)S(1)} %pad_add_fusion.here_ref, s32[64]{0:T(128)} %bitcast.34, bf16[8,64]{1,0:T(8,128)(2,1)} %bitcast.29, ...), custom_call_target="tpu_custom_call" | custom-call | bytes 6291456 | tf_op jit(solution)/shard_map/pack/pallas_call | solution.py:151
  6.4 1.9 %collective-permute-start.2 = (bf16[4,2,528,128]{3,2,1,0:T(8,128)(2,1)}, bf16[4,2,528,128]{3,2,1,0:T(8,128)(2,1)S(1)}, u32[]{:S(2)}, u32[]{:S(2)}) collective-permute-start(bf16[4,2,528,128]{3,2,1,0:T(8,128)(2,1)} %get-tuple-element.11), channel_id=1, source_target_pairs={{0,8},{8,0},{1,9},{9,1},{2,10},{10,2},{3,11},{11,3},{4,12},{12,4},... | collective-permute-start | bytes 3244040 | tf_op jit(solution)/shard_map/ppermute | solution.py:447
  8.3 0.2 slice_reduce_fusion.3
  8.5 0.2 slice_reduce_fusion.4
  8.8 2.4 %collective-permute-start = (f32[3,64]{1,0:T(4,128)S(1)}, f32[3,64]{1,0:T(4,128)S(1)}, u32[]{:S(2)}, u32[]{:S(2)}) collective-permute-start(f32[3,64]{1,0:T(4,128)S(1)} %pad_maximum_fusion), channel_id=1, source_target_pairs={{0,8},{8,16},{16,24},{24,32},{32,40},{40,48},{48,56},{1,9},{9,17},... | collective-permute-start | bytes 2312 | tf_op jit(solution)/shard_map/ppermute | solution.py:36
  11.2 1.3 %collective-permute-start.1 = (f32[3,64]{1,0:T(4,128)S(1)}, f32[3,64]{1,0:T(4,128)S(1)}, u32[]{:S(2)}, u32[]{:S(2)}) collective-permute-start(f32[3,64]{1,0:T(4,128)S(1)} %pad_maximum_fusion.1), channel_id=1, source_target_pairs={{8,0},{16,8},{24,16},{32,24},{40,32},{48,40},{56,48},{9,1},{17,9},... | collective-permute-start | bytes 2312 | tf_op jit(solution)/shard_map/ppermute | solution.py:36
  12.5 0.1 pad.6.clone
  12.6 0.0 collective-permute-done
  12.6 3.2 %collective-permute-done.1 = f32[3,64]{1,0:T(4,128)S(1)} collective-permute-done((f32[3,64]{1,0:T(4,128)S(1)}, f32[3,64]{1,0:T(4,128)S(1)}, u32[]{:S(2)}, u32[]{:S(2)}) %collective-permute-start.1) | collective-permute-done | bytes 800 | tf_op jit(solution)/shard_map/ppermute | solution.py:36
  15.8 0.1 maximum_maximum_fusion.rows_ref
  15.8 0.9 copies.1
  16.7 7.1 %all-to-all-start = ((f32[8,136,128]{2,1,0:T(8,128)}), f32[8,136,128]{2,1,0:T(8,128)S(1)}, u32[]{:S(2)}, u32[]{:S(2)}) async-start(f32[8,136,128]{2,1,0:T(8,128)} %copies.1), calls=%async_computation | async-start | bytes 1114112 | tf_op jit(solution)/shard_map/all_to_all | solution.py:457
  23.8 0.0 collective-permute-done.2.refs_3_.swapped_ref
  23.8 1.8 %join.1 = (bf16[4,528,128]{2,1,0:T(8,128)(2,1)}, bf16[4,528,128]{2,1,0:T(8,128)(2,1)}, bf16[4,528,128]{2,1,0:T(8,128)(2,1)}) custom-call(s32[2]{0:T(128)S(1)} %pad_add_fusion.here_ref, bf16[4,2,528,128]{3,2,1,0:T(8,128)(2,1)S(1)} %collective-permute-done.2.refs_3_.swapped_ref, bf16[2,528,128]{2,1,0:T(8,128)(2,1)S(1)} %get-tuple-element.12.first_own, ...), custom_call_target="tpu_custom_call" | custom-call | bytes 2097152 | tf_op jit(solution)/shard_map/join/pallas_call | solution.py:184
  25.6 6.1 %collective-permute-start.3 = (bf16[4,528,128]{2,1,0:T(8,128)(2,1)}, bf16[4,528,128]{2,1,0:T(8,128)(2,1)S(1)}, u32[]{:S(2)}, u32[]{:S(2)}) collective-permute-start(bf16[4,528,128]{2,1,0:T(8,128)(2,1)} %get-tuple-element.15), channel_id=1, source_target_pairs={{0,32},{4,36},{8,44},{12,40},{16,48},{20,52},{24,60},{28,56},{32,4... | collective-permute-start | bytes 1622024 | tf_op jit(solution)/shard_map/ppermute | solution.py:30
  31.7 4.2 %collective-permute-start.4 = (bf16[4,528,128]{2,1,0:T(8,128)(2,1)}, bf16[4,528,128]{2,1,0:T(8,128)(2,1)S(1)}, u32[]{:S(2)}, u32[]{:S(2)}) collective-permute-start(bf16[4,528,128]{2,1,0:T(8,128)(2,1)} %get-tuple-element.16), channel_id=1, source_target_pairs={{0,16},{4,20},{8,60},{12,56},{16,32},{20,36},{24,8},{28,12},{32,48... | collective-permute-start | bytes 1622024 | tf_op jit(solution)/shard_map/ppermute | solution.py:30
  35.9 4.4 %collective-permute-start.5 = (bf16[4,528,128]{2,1,0:T(8,128)(2,1)}, bf16[4,528,128]{2,1,0:T(8,128)(2,1)S(1)}, u32[]{:S(2)}, u32[]{:S(2)}) collective-permute-start(bf16[4,528,128]{2,1,0:T(8,128)(2,1)} %get-tuple-element.17), channel_id=1, source_target_pairs={{0,52},{4,48},{8,24},{12,28},{16,0},{20,4},{24,40},{28,44},{32,16}... | collective-permute-start | bytes 1622024 | tf_op jit(solution)/shard_map/ppermute | solution.py:30
  40.3 3.0 %all-to-all-done.got_ref = f32[8,136,128]{2,1,0:T(8,128)S(1)} async-done(((f32[8,136,128]{2,1,0:T(8,128)}), f32[8,136,128]{2,1,0:T(8,128)S(1)}, u32[]{:S(2)}, u32[]{:S(2)}) %all-to-all-start) | async-done | bytes 557088 | tf_op jit(solution)/shard_map/all_to_all | solution.py:457
  43.3 0.4 maps.1.refs_1_
  43.7 3.3 %shard_map.68.refs_2_ = f32[4,520,128]{2,1,0:T(8,128)S(1)} custom-call(s32[1]{0:T(128)} %bitcast.column_ref.refs_0_, f32[4,520,128]{2,1,0:T(8,128)S(1)} %maps.1.refs_1_, bf16[2,528,128]{2,1,0:T(8,128)(2,1)S(1)} %get-tuple-element.10.refs_2_, bf16[4,2,528,128]{3,2,1,0:T(8,128)(2,1)S(1)} %collective-permute-done.2.refs_3_.swapped_ref), custom_call_target="tpu_custom_call" | custom-call | flops 15974400 | bytes 4194304 | tf_op jit(solution)/shard_map/pallas_call | solution.py:415
  47.0 0.0 collective-permute-done.3.refs_3_
  47.0 3.3 %shard_map.69.refs_2_ = f32[4,520,128]{2,1,0:T(8,128)S(1)} custom-call(s32[1]{0:T(128)} %bitcast.column_ref.refs_0_, f32[4,520,128]{2,1,0:T(8,128)S(1)} %maps.1.refs_1_, f32[4,520,128]{2,1,0:T(8,128)S(1)} %shard_map.68.refs_2_, bf16[4,528,128]{2,1,0:T(8,128)(2,1)S(1)} %collective-permute-done.3.refs_3_), custom_call_target="tpu_custom_call" | custom-call | flops 15974400 | bytes 4194304 | tf_op jit(solution)/shard_map/pallas_call | solution.py:415
  50.3 11.0 %collective-permute-done.4.refs_3_ = bf16[4,528,128]{2,1,0:T(8,128)(2,1)S(1)} collective-permute-done((bf16[4,528,128]{2,1,0:T(8,128)(2,1)}, bf16[4,528,128]{2,1,0:T(8,128)(2,1)S(1)}, u32[]{:S(2)}, u32[]{:S(2)}) %collective-permute-start.4) | collective-permute-done | bytes 540704 | tf_op jit(solution)/shard_map/ppermute | solution.py:30
  61.4 3.3 %shard_map.70.refs_2_ = f32[4,520,128]{2,1,0:T(8,128)S(1)} custom-call(s32[1]{0:T(128)} %bitcast.column_ref.refs_0_, f32[4,520,128]{2,1,0:T(8,128)S(1)} %maps.1.refs_1_, f32[4,520,128]{2,1,0:T(8,128)S(1)} %shard_map.69.refs_2_, bf16[4,528,128]{2,1,0:T(8,128)(2,1)S(1)} %collective-permute-done.4.refs_3_), custom_call_target="tpu_custom_call" | custom-call | flops 15974400 | bytes 4194304 | tf_op jit(solution)/shard_map/pallas_call | solution.py:415
  64.7 0.0 collective-permute-done.5.refs_3_
  64.7 4.1 %shard_map.71 = f32[64,16,128]{2,1,0:T(8,128)S(1)} custom-call(s32[1]{0:T(128)} %bitcast.column_ref.refs_0_, f32[4,520,128]{2,1,0:T(8,128)S(1)} %maps.1.refs_1_, f32[4,520,128]{2,1,0:T(8,128)S(1)} %shard_map.70.refs_2_, bf16[4,528,128]{2,1,0:T(8,128)(2,1)S(1)} %collective-permute-done.5.refs_3_), custom_call_target="tpu_custom_call" | custom-call | flops 15974400 | bytes 4194304 | tf_op jit(solution)/shard_map/pallas_call | solution.py:415
  68.8 33.2 %all_to_all.10 = f32[64,16,128]{2,1,0:T(8,128)S(1)} all-to-all(f32[64,16,128]{2,1,0:T(8,128)S(1)} %shard_map.71), channel_id=1, replica_groups=mesh['y'=8,'zl'=4,'c'=2,'zh'=2,'x'=4] {'y','zh','x'}, dimensions={0} | all-to-all | bytes 1048576 | tf_op jit(solution)/shard_map/all_to_all | solution.py:465
  102.0 0.1 reduce_sum.9
  102.1 0.6 slice_bitcast_fusion
  (5 shorter events, 0.0 us)
Async XLA Ops:
  0.6 7.7 %copy-start.1 = (f32[1,64,128]{2,1,0:T(8,128)S(1)}, f32[1,64,128]{2,1,0:T(8,128)}, u32[]{:S(2)}) copy-start(f32[1,64,128]{2,1,0:T(8,128)} %param.6) | copy-start | bytes 98308
  0.6 7.9 %copy-start = (f32[1,64,128]{2,1,0:T(8,128)S(1)}, f32[1,64,128]{2,1,0:T(8,128)}, u32[]{:S(2)}) copy-start(f32[1,64,128]{2,1,0:T(8,128)} %param.5) | copy-start | bytes 98308
  6.4 17.4 %collective-permute-start.2 = (bf16[4,2,528,128]{3,2,1,0:T(8,128)(2,1)}, bf16[4,2,528,128]{3,2,1,0:T(8,128)(2,1)S(1)}, u32[]{:S(2)}, u32[]{:S(2)}) collective-permute-start(bf16[4,2,528,128]{3,2,1,0:T(8,128)(2,1)} %get-tuple-element.11), channel_id=1, source_target_pairs={{0,8},{8,0},{1,9},{9,1},{2,10},{10,2},{3,11},{11,3},{4,12},{12,4},... | collective-permute-start | bytes 3244040 | tf_op jit(solution)/shard_map/ppermute | solution.py:447
  8.8 3.8 %collective-permute-start = (f32[3,64]{1,0:T(4,128)S(1)}, f32[3,64]{1,0:T(4,128)S(1)}, u32[]{:S(2)}, u32[]{:S(2)}) collective-permute-start(f32[3,64]{1,0:T(4,128)S(1)} %pad_maximum_fusion), channel_id=1, source_target_pairs={{0,8},{8,16},{16,24},{24,32},{32,40},{40,48},{48,56},{1,9},{9,17},... | collective-permute-start | bytes 2312 | tf_op jit(solution)/shard_map/ppermute | solution.py:36
  11.2 4.6 %collective-permute-start.1 = (f32[3,64]{1,0:T(4,128)S(1)}, f32[3,64]{1,0:T(4,128)S(1)}, u32[]{:S(2)}, u32[]{:S(2)}) collective-permute-start(f32[3,64]{1,0:T(4,128)S(1)} %pad_maximum_fusion.1), channel_id=1, source_target_pairs={{8,0},{16,8},{24,16},{32,24},{40,32},{48,40},{56,48},{9,1},{17,9},... | collective-permute-start | bytes 2312 | tf_op jit(solution)/shard_map/ppermute | solution.py:36
  16.7 26.6 %all-to-all-start = ((f32[8,136,128]{2,1,0:T(8,128)}), f32[8,136,128]{2,1,0:T(8,128)S(1)}, u32[]{:S(2)}, u32[]{:S(2)}) async-start(f32[8,136,128]{2,1,0:T(8,128)} %copies.1), calls=%async_computation | async-start | bytes 1114112 | tf_op jit(solution)/shard_map/all_to_all | solution.py:457
  25.6 21.4 %collective-permute-start.3 = (bf16[4,528,128]{2,1,0:T(8,128)(2,1)}, bf16[4,528,128]{2,1,0:T(8,128)(2,1)S(1)}, u32[]{:S(2)}, u32[]{:S(2)}) collective-permute-start(bf16[4,528,128]{2,1,0:T(8,128)(2,1)} %get-tuple-element.15), channel_id=1, source_target_pairs={{0,32},{4,36},{8,44},{12,40},{16,48},{20,52},{24,60},{28,56},{32,4... | collective-permute-start | bytes 1622024 | tf_op jit(solution)/shard_map/ppermute | solution.py:30
  31.7 29.7 %collective-permute-start.4 = (bf16[4,528,128]{2,1,0:T(8,128)(2,1)}, bf16[4,528,128]{2,1,0:T(8,128)(2,1)S(1)}, u32[]{:S(2)}, u32[]{:S(2)}) collective-permute-start(bf16[4,528,128]{2,1,0:T(8,128)(2,1)} %get-tuple-element.16), channel_id=1, source_target_pairs={{0,16},{4,20},{8,60},{12,56},{16,32},{20,36},{24,8},{28,12},{32,48... | collective-permute-start | bytes 1622024 | tf_op jit(solution)/shard_map/ppermute | solution.py:30
  35.9 28.8 %collective-permute-start.5 = (bf16[4,528,128]{2,1,0:T(8,128)(2,1)}, bf16[4,528,128]{2,1,0:T(8,128)(2,1)S(1)}, u32[]{:S(2)}, u32[]{:S(2)}) collective-permute-start(bf16[4,528,128]{2,1,0:T(8,128)(2,1)} %get-tuple-element.17), channel_id=1, source_target_pairs={{0,52},{4,48},{8,24},{12,28},{16,0},{20,4},{24,40},{28,44},{32,16}... | collective-permute-start | bytes 1622024 | tf_op jit(solution)/shard_map/ppermute | solution.py:30
where the time goes:
time: 103 us
  blocking collectives  33.2 us (32%)
  starting transfers between devices  27.4 us (27%)
  Pallas kernels  22.8 us (22%)
  waiting for transfers between devices  17.2 us (17%)
  local copies, waits for them, and re-layouts  1.08 us (1%)
    all_to_all x1, blocking collectives, body(): lax.all_to_all(parts, ('y',) + IMG, split_axis=0, concat_axis=0, tiled=True)  33.2 us
    ppermute x3, starting transfers between devices, ring_shift(): return lax.ppermute(value, ('zl', 'c', 'zh'), pairs)  14.7 us
    pallas_call x4, Pallas kernels, terms(): pl.pallas_call(lambda *refs: terms_kernel(scale, sums is not None, picks,...  14 us
    ppermute x3, waiting for transfers between devices, ring_shift(): return lax.ppermute(value, ('zl', 'c', 'zh'), pairs)  11 us
    all_to_all x1, starting transfers between devices, body(): lax.all_to_all(copies, 'y', split_axis=0, concat_axis=0, tiled=True)  7.1 us
    pallas_call x1, Pallas kernels, pack(): pl.pallas_call(pack_kernel, out_shape=[pltpu.VMEM(lead + unit, jnp.bfloat...  5.67 us
    ppermute x2, starting transfers between devices, column_shift(): return lax.ppermute(value, ('zl', 'c'), pairs)  3.69 us
    ppermute x2, waiting for transfers between devices, column_shift(): return lax.ppermute(value, ('zl', 'c'), pairs)  3.17 us
  transfers between devices with their start and end apart: 7, of which 3 were waited for; matrix products, arithmetic and copies ran while one was open for 1% of the time, Pallas kernels for 13%

commit v1 on v0

--- a/solution.py
+++ b/solution.py
@@ -10,6 +10,7 @@
 SMOOTH = 0.0025
 PARAMS = 8
 STRIP = 16
+PLACED = 2
 ROWS, CLASSES, CORES, HALVES, DEPTH = 8, 4, 2, 2, 4
 RING = CLASSES * HALVES
 TILE = ("y", "zl", "c")
@@ -121,7 +122,8 @@
 
             def place(step, carry):
                 found = []
-                for row in (step * 2, step * 2 + 1):
+                for row in range(PLACED):
+                    row = step * PLACED + row
                     tile = row * count + column
                     for slot in (0, 1):
                         block = table[2 * tile + slot]
@@ -130,7 +132,7 @@
                             column < count - 1, table[jnp.minimum(2 * tile + 2, 2 * ROWS * count - 2) + slot], number
                         )
                         line = shifted[0, pl.ds(block, 1), :] + shifted[1, pl.ds(west, 1), :] + shifted[2, pl.ds(east, 1), :]
-                        sides = [rim[index % 2, pl.ds(index // 2, 1), :] for index in (west, east)]
+                        sides = [rim[index & 1, pl.ds(index >> 1, 1), :] for index in (west, east)]
                         found.append((row, slot, blocks_ref[block], jnp.where(west_half, sides[0], sides[1]), line))
                 for row, slot, values, side, line in found:
                     start = pl.multiple_of(row * tile_rows, tile_rows)
@@ -139,7 +141,7 @@
                     lines[1, slot, pl.ds(row, 1), :] = line
                 return carry
 
-            lax.fori_loop(0, ROWS // 2, place, 0)
+            lax.fori_loop(0, ROWS // PLACED, place, 0)
             for slot in (0, 1):
                 for k in (0, 1):
                     units[slot][pixels + k * ROWS : pixels + (k + 1) * ROWS, :] = lines[k, slot].astype(jnp.bfloat16)
@@ -458,8 +460,7 @@
     column = column_here.reshape(1).astype(jnp.int32)
     maps = make_maps(column, gathered)
 
-    sums = terms(column, maps, None, [(near, [(0,), (1,)]), (swapped, [(0, 0), (0, 1)])], None)
-    sums = terms(column, maps, sums, [(far, EACH4)], None)
+    sums = terms(column, maps, None, [(near, EACH2), (swapped, [(0, 0), (0, 1)]), (far, EACH4)], None)
     sums = terms(column, maps, sums, [(next0, EACH4)], None)
     parts = terms(column, maps, sums, [(next1, EACH4)], 1.0 / block_count)
     summed = jnp.sum(lax.all_to_all(parts, ("y",) + IMG, split_axis=0, concat_axis=0, tiled=True), axis=0)

time: 103 us -> 102 us (level)
  Pallas kernels: 22.8 us -> 20.6 us
    pallas_call x1, Pallas kernels: 5.67 us -> 4.55 us  [pack(): pl.pallas_call(pack_kernel, out_shape=[pltpu.VMEM(lead + unit, jnp.bfloat...]
    pallas_call x4 -> x3, Pallas kernels: 14 us -> 13 us  [terms(): pl.pallas_call(lambda *refs: terms_kernel(scale, sums is not None, picks,...]
  transfers between devices with their start and end apart: 7 -> 7, of which waited for: 3 -> 4; matrix products, arithmetic and copies ran while one was open for 1% -> 1% of each run, Pallas kernels for 13% -> 12%
where the time goes in v1:
time: 102 us
  blocking collectives  33.2 us (33%)
  starting transfers between devices  27.4 us (27%)
  Pallas kernels  20.6 us (20%)
  waiting for transfers between devices  18.2 us (18%)
  local copies, waits for them, and re-layouts  1.08 us (1%)
    all_to_all x1, blocking collectives, body(): lax.all_to_all(parts, ('y',) + IMG, split_axis=0, concat_axis=0, tiled=True)  33.2 us
    ppermute x3, starting transfers between devices, ring_shift(): return lax.ppermute(value, ('zl', 'c', 'zh'), pairs)  14.7 us
    pallas_call x3, Pallas kernels, terms(): pl.pallas_call(lambda *refs: terms_kernel(scale, sums is not None, picks,...  13 us
    ppermute x3, waiting for transfers between devices, ring_shift(): return lax.ppermute(value, ('zl', 'c', 'zh'), pairs)  12.1 us
    all_to_all x1, starting transfers between devices, body(): lax.all_to_all(copies, 'y', split_axis=0, concat_axis=0, tiled=True)  7.1 us
    pallas_call x1, Pallas kernels, pack(): pl.pallas_call(pack_kernel, out_shape=[pltpu.VMEM(lead + unit, jnp.bfloat...  4.55 us
    ppermute x2, starting transfers between devices, column_shift(): return lax.ppermute(value, ('zl', 'c'), pairs)  3.69 us
    ppermute x2, waiting for transfers between devices, column_shift(): return lax.ppermute(value, ('zl', 'c'), pairs)  3.17 us
  transfers between devices with their start and end apart: 7, of which 4 were waited for; matrix products, arithmetic and copies ran while one was open for 1% of the time, Pallas kernels for 12%

profile of v1, /device:TPU:6, one launch (start us, length us, event | category | flops | bytes accessed | tf_op | source)
XLA Modules:
  0.0 101.6 jit_solution(10804308993414766167)
XLA Ops:
  0.6 0.0 copy-start.1
  0.6 0.0 copy-start
  0.7 0.1 pad_add_fusion.here_ref
  0.7 4.5 %pack.1 = (bf16[2,528,128]{2,1,0:T(8,128)(2,1)S(1)}, bf16[2,528,128]{2,1,0:T(8,128)(2,1)S(1)}, bf16[2,528,128]{2,1,0:T(8,128)(2,1)S(1)}, bf16[2,528,128]{2,1,0:T(8,128)(2,1)S(1)}, bf16[4,2,528,128]{3,2,1,0:T(8,128)(2,1)}) custom-call(s32[2]{0:T(128)S(1)} %pad_add_fusion.here_ref, s32[64]{0:T(128)} %bitcast.34, bf16[8,64]{1,0:T(8,128)(2,1)} %bitcast.29, ...), custom_call_target="tpu_custom_call" | custom-call | bytes 6291456 | tf_op jit(solution)/shard_map/pack/pallas_call | solution.py:153
  5.3 1.9 %collective-permute-start.2 = (bf16[4,2,528,128]{3,2,1,0:T(8,128)(2,1)}, bf16[4,2,528,128]{3,2,1,0:T(8,128)(2,1)S(1)}, u32[]{:S(2)}, u32[]{:S(2)}) collective-permute-start(bf16[4,2,528,128]{3,2,1,0:T(8,128)(2,1)} %get-tuple-element.11), channel_id=1, source_target_pairs={{0,8},{8,0},{1,9},{9,1},{2,10},{10,2},{3,11},{11,3},{4,12},{12,4},... | collective-permute-start | bytes 3244040 | tf_op jit(solution)/shard_map/ppermute | solution.py:449
  7.2 0.2 slice_reduce_fusion.3
  7.4 0.0 copy-done
  7.4 0.2 slice_reduce_fusion.4
  7.7 2.4 %collective-permute-start = (f32[3,64]{1,0:T(4,128)S(1)}, f32[3,64]{1,0:T(4,128)S(1)}, u32[]{:S(2)}, u32[]{:S(2)}) collective-permute-start(f32[3,64]{1,0:T(4,128)S(1)} %pad_maximum_fusion), channel_id=1, source_target_pairs={{0,8},{8,16},{16,24},{24,32},{32,40},{40,48},{48,56},{1,9},{9,17},... | collective-permute-start | bytes 2312 | tf_op jit(solution)/shard_map/ppermute | solution.py:37
  10.1 1.3 %collective-permute-start.1 = (f32[3,64]{1,0:T(4,128)S(1)}, f32[3,64]{1,0:T(4,128)S(1)}, u32[]{:S(2)}, u32[]{:S(2)}) collective-permute-start(f32[3,64]{1,0:T(4,128)S(1)} %pad_maximum_fusion.1), channel_id=1, source_target_pairs={{8,0},{16,8},{24,16},{32,24},{40,32},{48,40},{56,48},{9,1},{17,9},... | collective-permute-start | bytes 2312 | tf_op jit(solution)/shard_map/ppermute | solution.py:37
  11.4 0.1 pad.6.clone
  11.5 0.0 collective-permute-done
  11.5 3.2 %collective-permute-done.1 = f32[3,64]{1,0:T(4,128)S(1)} collective-permute-done((f32[3,64]{1,0:T(4,128)S(1)}, f32[3,64]{1,0:T(4,128)S(1)}, u32[]{:S(2)}, u32[]{:S(2)}) %collective-permute-start.1) | collective-permute-done | bytes 800 | tf_op jit(solution)/shard_map/ppermute | solution.py:37
  14.6 0.1 maximum_maximum_fusion.rows_ref
  14.7 0.9 copies.1
  15.6 7.1 %all-to-all-start = ((f32[8,136,128]{2,1,0:T(8,128)}), f32[8,136,128]{2,1,0:T(8,128)S(1)}, u32[]{:S(2)}, u32[]{:S(2)}) async-start(f32[8,136,128]{2,1,0:T(8,128)} %copies.1), calls=%async_computation | async-start | bytes 1114112 | tf_op jit(solution)/shard_map/all_to_all | solution.py:459
  22.7 0.0 collective-permute-done.2.swapped_ref.refs_3_
  22.7 1.8 %join.1 = (bf16[4,528,128]{2,1,0:T(8,128)(2,1)}, bf16[4,528,128]{2,1,0:T(8,128)(2,1)}, bf16[4,528,128]{2,1,0:T(8,128)(2,1)}) custom-call(s32[2]{0:T(128)S(1)} %pad_add_fusion.here_ref, bf16[4,2,528,128]{3,2,1,0:T(8,128)(2,1)S(1)} %collective-permute-done.2.swapped_ref.refs_3_, bf16[2,528,128]{2,1,0:T(8,128)(2,1)S(1)} %get-tuple-element.12.first_own, ...), custom_call_target="tpu_custom_call" | custom-call | bytes 2097152 | tf_op jit(solution)/shard_map/join/pallas_call | solution.py:186
  24.5 6.1 %collective-permute-start.3 = (bf16[4,528,128]{2,1,0:T(8,128)(2,1)}, bf16[4,528,128]{2,1,0:T(8,128)(2,1)S(1)}, u32[]{:S(2)}, u32[]{:S(2)}) collective-permute-start(bf16[4,528,128]{2,1,0:T(8,128)(2,1)} %get-tuple-element.15), channel_id=1, source_target_pairs={{0,32},{4,36},{8,44},{12,40},{16,48},{20,52},{24,60},{28,56},{32,4... | collective-permute-start | bytes 1622024 | tf_op jit(solution)/shard_map/ppermute | solution.py:31
  30.6 4.2 %collective-permute-start.4 = (bf16[4,528,128]{2,1,0:T(8,128)(2,1)}, bf16[4,528,128]{2,1,0:T(8,128)(2,1)S(1)}, u32[]{:S(2)}, u32[]{:S(2)}) collective-permute-start(bf16[4,528,128]{2,1,0:T(8,128)(2,1)} %get-tuple-element.16), channel_id=1, source_target_pairs={{0,16},{4,20},{8,60},{12,56},{16,32},{20,36},{24,8},{28,12},{32,48... | collective-permute-start | bytes 1622024 | tf_op jit(solution)/shard_map/ppermute | solution.py:31
  34.8 4.4 %collective-permute-start.5 = (bf16[4,528,128]{2,1,0:T(8,128)(2,1)}, bf16[4,528,128]{2,1,0:T(8,128)(2,1)S(1)}, u32[]{:S(2)}, u32[]{:S(2)}) collective-permute-start(bf16[4,528,128]{2,1,0:T(8,128)(2,1)} %get-tuple-element.17), channel_id=1, source_target_pairs={{0,52},{4,48},{8,24},{12,28},{16,0},{20,4},{24,40},{28,44},{32,16}... | collective-permute-start | bytes 1622024 | tf_op jit(solution)/shard_map/ppermute | solution.py:31
  39.2 3.0 %all-to-all-done.got_ref = f32[8,136,128]{2,1,0:T(8,128)S(1)} async-done(((f32[8,136,128]{2,1,0:T(8,128)}), f32[8,136,128]{2,1,0:T(8,128)S(1)}, u32[]{:S(2)}, u32[]{:S(2)}) %all-to-all-start) | async-done | bytes 557088 | tf_op jit(solution)/shard_map/all_to_all | solution.py:459
  42.2 0.4 maps.1.refs_1_
  42.6 0.4 collective-permute-done.3.refs_4_
  43.1 5.6 %shard_map.68.refs_2_ = f32[4,520,128]{2,1,0:T(8,128)S(1)} custom-call(s32[1]{0:T(128)} %bitcast.column_ref.refs_0_, f32[4,520,128]{2,1,0:T(8,128)S(1)} %maps.1.refs_1_, bf16[2,528,128]{2,1,0:T(8,128)(2,1)S(1)} %get-tuple-element.10.refs_2_, bf16[4,2,528,128]{3,2,1,0:T(8,128)(2,1)S(1)} %collective-permute-done.2.swapped_ref.refs_3_, ...), custom_call_target="tpu_custom_call" | custom-call | flops 31948800 | bytes 4194304 | tf_op jit(solution)/shard_map/pallas_call | solution.py:417
  48.6 11.6 %collective-permute-done.4.refs_3_ = bf16[4,528,128]{2,1,0:T(8,128)(2,1)S(1)} collective-permute-done((bf16[4,528,128]{2,1,0:T(8,128)(2,1)}, bf16[4,528,128]{2,1,0:T(8,128)(2,1)S(1)}, u32[]{:S(2)}, u32[]{:S(2)}) %collective-permute-start.4) | collective-permute-done | bytes 540704 | tf_op jit(solution)/shard_map/ppermute | solution.py:31
  60.3 3.3 %shard_map.69.refs_2_ = f32[4,520,128]{2,1,0:T(8,128)S(1)} custom-call(s32[1]{0:T(128)} %bitcast.column_ref.refs_0_, f32[4,520,128]{2,1,0:T(8,128)S(1)} %maps.1.refs_1_, f32[4,520,128]{2,1,0:T(8,128)S(1)} %shard_map.68.refs_2_, bf16[4,528,128]{2,1,0:T(8,128)(2,1)S(1)} %collective-permute-done.4.refs_3_), custom_call_target="tpu_custom_call" | custom-call | flops 15974400 | bytes 4194304 | tf_op jit(solution)/shard_map/pallas_call | solution.py:417
  63.6 0.0 collective-permute-done.5.refs_3_
  63.6 4.1 %shard_map.70 = f32[64,16,128]{2,1,0:T(8,128)S(1)} custom-call(s32[1]{0:T(128)} %bitcast.column_ref.refs_0_, f32[4,520,128]{2,1,0:T(8,128)S(1)} %maps.1.refs_1_, f32[4,520,128]{2,1,0:T(8,128)S(1)} %shard_map.69.refs_2_, bf16[4,528,128]{2,1,0:T(8,128)(2,1)S(1)} %collective-permute-done.5.refs_3_), custom_call_target="tpu_custom_call" | custom-call | flops 15974400 | bytes 4194304 | tf_op jit(solution)/shard_map/pallas_call | solution.py:417
  67.7 33.2 %all_to_all.10 = f32[64,16,128]{2,1,0:T(8,128)S(1)} all-to-all(f32[64,16,128]{2,1,0:T(8,128)S(1)} %shard_map.70), channel_id=1, replica_groups=mesh['y'=8,'zl'=4,'c'=2,'zh'=2,'x'=4] {'y','zh','x'}, dimensions={0} | all-to-all | bytes 1048576 | tf_op jit(solution)/shard_map/all_to_all | solution.py:466
  100.9 0.1 reduce_sum.9
  101.0 0.6 slice_bitcast_fusion
  (4 shorter events, 0.0 us)
Async XLA Ops:
  0.6 6.6 %copy-start.1 = (f32[1,64,128]{2,1,0:T(8,128)S(1)}, f32[1,64,128]{2,1,0:T(8,128)}, u32[]{:S(2)}) copy-start(f32[1,64,128]{2,1,0:T(8,128)} %param.6) | copy-start | bytes 98308
  0.6 6.8 %copy-start = (f32[1,64,128]{2,1,0:T(8,128)S(1)}, f32[1,64,128]{2,1,0:T(8,128)}, u32[]{:S(2)}) copy-start(f32[1,64,128]{2,1,0:T(8,128)} %param.5) | copy-start | bytes 98308
  5.3 17.4 %collective-permute-start.2 = (bf16[4,2,528,128]{3,2,1,0:T(8,128)(2,1)}, bf16[4,2,528,128]{3,2,1,0:T(8,128)(2,1)S(1)}, u32[]{:S(2)}, u32[]{:S(2)}) collective-permute-start(bf16[4,2,528,128]{3,2,1,0:T(8,128)(2,1)} %get-tuple-element.11), channel_id=1, source_target_pairs={{0,8},{8,0},{1,9},{9,1},{2,10},{10,2},{3,11},{11,3},{4,12},{12,4},... | collective-permute-start | bytes 3244040 | tf_op jit(solution)/shard_map/ppermute | solution.py:449
  7.7 3.8 %collective-permute-start = (f32[3,64]{1,0:T(4,128)S(1)}, f32[3,64]{1,0:T(4,128)S(1)}, u32[]{:S(2)}, u32[]{:S(2)}) collective-permute-start(f32[3,64]{1,0:T(4,128)S(1)} %pad_maximum_fusion), channel_id=1, source_target_pairs={{0,8},{8,16},{16,24},{24,32},{32,40},{40,48},{48,56},{1,9},{9,17},... | collective-permute-start | bytes 2312 | tf_op jit(solution)/shard_map/ppermute | solution.py:37
  10.1 4.6 %collective-permute-start.1 = (f32[3,64]{1,0:T(4,128)S(1)}, f32[3,64]{1,0:T(4,128)S(1)}, u32[]{:S(2)}, u32[]{:S(2)}) collective-permute-start(f32[3,64]{1,0:T(4,128)S(1)} %pad_maximum_fusion.1), channel_id=1, source_target_pairs={{8,0},{16,8},{24,16},{32,24},{40,32},{48,40},{56,48},{9,1},{17,9},... | collective-permute-start | bytes 2312 | tf_op jit(solution)/shard_map/ppermute | solution.py:37
  15.6 26.6 %all-to-all-start = ((f32[8,136,128]{2,1,0:T(8,128)}), f32[8,136,128]{2,1,0:T(8,128)S(1)}, u32[]{:S(2)}, u32[]{:S(2)}) async-start(f32[8,136,128]{2,1,0:T(8,128)} %copies.1), calls=%async_computation | async-start | bytes 1114112 | tf_op jit(solution)/shard_map/all_to_all | solution.py:459
  24.5 18.5 %collective-permute-start.3 = (bf16[4,528,128]{2,1,0:T(8,128)(2,1)}, bf16[4,528,128]{2,1,0:T(8,128)(2,1)S(1)}, u32[]{:S(2)}, u32[]{:S(2)}) collective-permute-start(bf16[4,528,128]{2,1,0:T(8,128)(2,1)} %get-tuple-element.15), channel_id=1, source_target_pairs={{0,32},{4,36},{8,44},{12,40},{16,48},{20,52},{24,60},{28,56},{32,4... | collective-permute-start | bytes 1622024 | tf_op jit(solution)/shard_map/ppermute | solution.py:31
  30.6 29.7 %collective-permute-start.4 = (bf16[4,528,128]{2,1,0:T(8,128)(2,1)}, bf16[4,528,128]{2,1,0:T(8,128)(2,1)S(1)}, u32[]{:S(2)}, u32[]{:S(2)}) collective-permute-start(bf16[4,528,128]{2,1,0:T(8,128)(2,1)} %get-tuple-element.16), channel_id=1, source_target_pairs={{0,16},{4,20},{8,60},{12,56},{16,32},{20,36},{24,8},{28,12},{32,48... | collective-permute-start | bytes 1622024 | tf_op jit(solution)/shard_map/ppermute | solution.py:31
  34.8 28.8 %collective-permute-start.5 = (bf16[4,528,128]{2,1,0:T(8,128)(2,1)}, bf16[4,528,128]{2,1,0:T(8,128)(2,1)S(1)}, u32[]{:S(2)}, u32[]{:S(2)}) collective-permute-start(bf16[4,528,128]{2,1,0:T(8,128)(2,1)} %get-tuple-element.17), channel_id=1, source_target_pairs={{0,52},{4,48},{8,24},{12,28},{16,0},{20,4},{24,40},{28,44},{32,16}... | collective-permute-start | bytes 1622024 | tf_op jit(solution)/shard_map/ppermute | solution.py:31

commit v2 on v1

--- a/solution.py
+++ b/solution.py
@@ -31,10 +31,7 @@
     return lax.ppermute(value, ("zl", "c", "zh"), pairs)
 
 
-def column_shift(value, steps):
-    count = CLASSES * CORES
-    pairs = [(k, k + steps) for k in range(count) if 0 <= k + steps < count]
-    return lax.ppermute(value, ("zl", "c"), pairs)
+BETWEEN = [pair for k in range(1, CLASSES * CORES - 1, 2) for pair in ((k, k + 1), (k + 1, k))]
 
 
 def in_vmem(*arrays):
@@ -436,8 +433,11 @@
 
     height, shade = heights[0], albedo[0]
     first, last = jnp.stack([height[:, 0], height[:, 1], shade[:, 0]]), jnp.stack([height[:, -1], height[:, -2], shade[:, -1]])
-    from_west = column_shift(last, 1)
-    from_east = column_shift(first, -1)
+    even = lax.axis_index("c") == 0
+    inward, outward = jnp.where(even, last, first), jnp.where(even, first, last)
+    across = lax.ppermute(inward, "c", [(0, 1), (1, 0)])
+    beyond = lax.ppermute(outward, ("zl", "c"), BETWEEN)
+    from_west, from_east = jnp.where(even, beyond, across), jnp.where(even, across, beyond)
 
     here = jnp.stack([lax.axis_index("zl"), lax.axis_index("c")]).astype(jnp.int32)
     near, *own, other = pack(

time: 102 us -> 100 us (0.980)
  waiting for transfers between devices: 18.2 us -> 15.8 us
  starting transfers between devices: 27.4 us -> 28.6 us
    ppermute x2, starting transfers between devices: 3.69 us -> 6.3 us  [the longest x1 5.64 us: body(): across = lax.ppermute(inward, 'c', [(0, 1), (1, 0)])]
    ppermute x2, waiting for transfers between devices: 3.17 us -> 0.71 us  [the longest x1 0.71 us: body(): across = lax.ppermute(inward, 'c', [(0, 1), (1, 0)])]
    ppermute x3, starting transfers between devices: 14.7 us -> 13.3 us  [ring_shift(): return lax.ppermute(value, ('zl', 'c', 'zh'), pairs)]
where the time goes in v2:
time: 100 us; the launch traced here: 99.7 us
  blocking collectives  32.6 us (33%)
  starting transfers between devices  28.6 us (29%)
  Pallas kernels  20.6 us (21%)
  waiting for transfers between devices  15.8 us (16%)
  local copies, waits for them, and re-layouts  1.08 us (1%)
    all_to_all x1, blocking collectives, body(): lax.all_to_all(parts, ('y',) + IMG, split_axis=0, concat_axis=0, tiled=True)  32.6 us
    ppermute x3, starting transfers between devices, ring_shift(): return lax.ppermute(value, ('zl', 'c', 'zh'), pairs)  13.3 us
    pallas_call x3, Pallas kernels, terms(): pl.pallas_call(lambda *refs: terms_kernel(scale, sums is not None, picks,...  13 us
    ppermute x3, waiting for transfers between devices, ring_shift(): return lax.ppermute(value, ('zl', 'c', 'zh'), pairs)  11.5 us
    all_to_all x1, starting transfers between devices, body(): lax.all_to_all(copies, 'y', split_axis=0, concat_axis=0, tiled=True)  7.1 us
    ppermute x1, starting transfers between devices, body(): across = lax.ppermute(inward, 'c', [(0, 1), (1, 0)])  5.64 us
    pallas_call x1, Pallas kernels, pack(): pl.pallas_call(pack_kernel, out_shape=[pltpu.VMEM(lead + unit, jnp.bfloat...  4.55 us
    all_to_all x1, waiting for transfers between devices, body(): lax.all_to_all(copies, 'y', split_axis=0, concat_axis=0, tiled=True)  3.59 us
  transfers between devices with their start and end apart: 7, of which 4 were waited for; matrix products, arithmetic and copies ran while one was open for 1% of the time, Pallas kernels for 12%

profile of v2, /device:TPU:6, one launch (start us, length us, event | category | flops | bytes accessed | tf_op | source)
XLA Modules:
  0.0 99.7 jit_solution(7145490147215673005)
XLA Ops:
  0.6 0.0 copy-start
  0.6 0.0 copy-start.1
  0.7 0.1 pad_add_fusion.here_ref
  0.7 4.5 %pack.1 = (bf16[2,528,128]{2,1,0:T(8,128)(2,1)S(1)}, bf16[2,528,128]{2,1,0:T(8,128)(2,1)S(1)}, bf16[2,528,128]{2,1,0:T(8,128)(2,1)S(1)}, bf16[2,528,128]{2,1,0:T(8,128)(2,1)S(1)}, bf16[4,2,528,128]{3,2,1,0:T(8,128)(2,1)}) custom-call(s32[2]{0:T(128)S(1)} %pad_add_fusion.here_ref, s32[64]{0:T(128)} %bitcast.34, bf16[8,64]{1,0:T(8,128)(2,1)} %bitcast.29, ...), custom_call_target="tpu_custom_call" | custom-call | bytes 6291456 | tf_op jit(solution)/shard_map/pack/pallas_call | solution.py:150
  5.3 1.9 %collective-permute-start.2 = (bf16[4,2,528,128]{3,2,1,0:T(8,128)(2,1)}, bf16[4,2,528,128]{3,2,1,0:T(8,128)(2,1)S(1)}, u32[]{:S(2)}, u32[]{:S(2)}) collective-permute-start(bf16[4,2,528,128]{3,2,1,0:T(8,128)(2,1)} %get-tuple-element.11), channel_id=1, source_target_pairs={{0,8},{8,0},{1,9},{9,1},{2,10},{10,2},{3,11},{11,3},{4,12},{12,4},... | collective-permute-start | bytes 3244040 | tf_op jit(solution)/shard_map/ppermute | solution.py:449
  7.2 0.0 copy-done
  7.2 0.2 slice_reduce_fusion.4
  7.5 0.2 slice_reduce_fusion.3
  7.7 0.7 collective-permute-start
  8.3 5.6 %collective-permute-start.1 = (f32[3,64]{1,0:T(4,128)S(1)}, f32[3,64]{1,0:T(4,128)S(1)}, u32[]{:S(2)}, u32[]{:S(2)}) collective-permute-start(f32[3,64]{1,0:T(4,128)S(1)} %get-tuple-element.29), channel_id=1, source_target_pairs={{0,8},{8,0},{1,9},{9,1},{2,10},{10,2},{3,11},{11,3},{4,12},{12,4},... | collective-permute-start | bytes 2312 | tf_op jit(solution)/shard_map/ppermute | solution.py:438
  14.0 0.1 pad.6.clone
  14.1 0.0 collective-permute-done
  14.1 0.7 collective-permute-done.1
  14.8 0.1 maximum_maximum_fusion.rows_ref
  14.9 0.9 copies.1
  15.7 7.1 %all-to-all-start = ((f32[8,136,128]{2,1,0:T(8,128)}), f32[8,136,128]{2,1,0:T(8,128)S(1)}, u32[]{:S(2)}, u32[]{:S(2)}) async-start(f32[8,136,128]{2,1,0:T(8,128)} %copies.1), calls=%async_computation | async-start | bytes 1114112 | tf_op jit(solution)/shard_map/all_to_all | solution.py:459
  22.8 0.0 collective-permute-done.2.swapped_ref.refs_3_
  22.8 1.8 %join.1 = (bf16[4,528,128]{2,1,0:T(8,128)(2,1)}, bf16[4,528,128]{2,1,0:T(8,128)(2,1)}, bf16[4,528,128]{2,1,0:T(8,128)(2,1)}) custom-call(s32[2]{0:T(128)S(1)} %pad_add_fusion.here_ref, bf16[4,2,528,128]{3,2,1,0:T(8,128)(2,1)S(1)} %collective-permute-done.2.swapped_ref.refs_3_, bf16[2,528,128]{2,1,0:T(8,128)(2,1)S(1)} %get-tuple-element.12.first_own, ...), custom_call_target="tpu_custom_call" | custom-call | bytes 2097152 | tf_op jit(solution)/shard_map/join/pallas_call | solution.py:183
  24.7 6.1 %collective-permute-start.3 = (bf16[4,528,128]{2,1,0:T(8,128)(2,1)}, bf16[4,528,128]{2,1,0:T(8,128)(2,1)S(1)}, u32[]{:S(2)}, u32[]{:S(2)}) collective-permute-start(bf16[4,528,128]{2,1,0:T(8,128)(2,1)} %get-tuple-element.15), channel_id=1, source_target_pairs={{0,32},{4,36},{8,44},{12,40},{16,48},{20,52},{24,60},{28,56},{32,4... | collective-permute-start | bytes 1622024 | tf_op jit(solution)/shard_map/ppermute | solution.py:31
  30.8 2.1 %collective-permute-start.4 = (bf16[4,528,128]{2,1,0:T(8,128)(2,1)}, bf16[4,528,128]{2,1,0:T(8,128)(2,1)S(1)}, u32[]{:S(2)}, u32[]{:S(2)}) collective-permute-start(bf16[4,528,128]{2,1,0:T(8,128)(2,1)} %get-tuple-element.16), channel_id=1, source_target_pairs={{0,16},{4,20},{8,60},{12,56},{16,32},{20,36},{24,8},{28,12},{32,48... | collective-permute-start | bytes 1622024 | tf_op jit(solution)/shard_map/ppermute | solution.py:31
  32.9 5.1 %collective-permute-start.5 = (bf16[4,528,128]{2,1,0:T(8,128)(2,1)}, bf16[4,528,128]{2,1,0:T(8,128)(2,1)S(1)}, u32[]{:S(2)}, u32[]{:S(2)}) collective-permute-start(bf16[4,528,128]{2,1,0:T(8,128)(2,1)} %get-tuple-element.17), channel_id=1, source_target_pairs={{0,52},{4,48},{8,24},{12,28},{16,0},{20,4},{24,40},{28,44},{32,16}... | collective-permute-start | bytes 1622024 | tf_op jit(solution)/shard_map/ppermute | solution.py:31
  38.0 3.6 %all-to-all-done.got_ref = f32[8,136,128]{2,1,0:T(8,128)S(1)} async-done(((f32[8,136,128]{2,1,0:T(8,128)}), f32[8,136,128]{2,1,0:T(8,128)S(1)}, u32[]{:S(2)}, u32[]{:S(2)}) %all-to-all-start) | async-done | bytes 557088 | tf_op jit(solution)/shard_map/all_to_all | solution.py:459
  41.6 0.4 maps.1.refs_1_
  42.0 4.6 %collective-permute-done.3.refs_4_ = bf16[4,528,128]{2,1,0:T(8,128)(2,1)S(1)} collective-permute-done((bf16[4,528,128]{2,1,0:T(8,128)(2,1)}, bf16[4,528,128]{2,1,0:T(8,128)(2,1)S(1)}, u32[]{:S(2)}, u32[]{:S(2)}) %collective-permute-start.3) | collective-permute-done | bytes 540704 | tf_op jit(solution)/shard_map/ppermute | solution.py:31
  46.6 5.6 %shard_map.68.refs_2_ = f32[4,520,128]{2,1,0:T(8,128)S(1)} custom-call(s32[1]{0:T(128)} %bitcast.column_ref.refs_0_, f32[4,520,128]{2,1,0:T(8,128)S(1)} %maps.1.refs_1_, bf16[2,528,128]{2,1,0:T(8,128)(2,1)S(1)} %get-tuple-element.10.refs_2_, bf16[4,2,528,128]{3,2,1,0:T(8,128)(2,1)S(1)} %collective-permute-done.2.swapped_ref.refs_3_, ...), custom_call_target="tpu_custom_call" | custom-call | flops 31948800 | bytes 4194304 | tf_op jit(solution)/shard_map/pallas_call | solution.py:414
  52.2 6.8 %collective-permute-done.4.refs_3_ = bf16[4,528,128]{2,1,0:T(8,128)(2,1)S(1)} collective-permute-done((bf16[4,528,128]{2,1,0:T(8,128)(2,1)}, bf16[4,528,128]{2,1,0:T(8,128)(2,1)S(1)}, u32[]{:S(2)}, u32[]{:S(2)}) %collective-permute-start.4) | collective-permute-done | bytes 540704 | tf_op jit(solution)/shard_map/ppermute | solution.py:31
  59.0 3.3 %shard_map.69.refs_2_ = f32[4,520,128]{2,1,0:T(8,128)S(1)} custom-call(s32[1]{0:T(128)} %bitcast.column_ref.refs_0_, f32[4,520,128]{2,1,0:T(8,128)S(1)} %maps.1.refs_1_, f32[4,520,128]{2,1,0:T(8,128)S(1)} %shard_map.68.refs_2_, bf16[4,528,128]{2,1,0:T(8,128)(2,1)S(1)} %collective-permute-done.4.refs_3_), custom_call_target="tpu_custom_call" | custom-call | flops 15974400 | bytes 4194304 | tf_op jit(solution)/shard_map/pallas_call | solution.py:414
  62.3 0.0 collective-permute-done.5.refs_3_
  62.4 4.1 %shard_map.70 = f32[64,16,128]{2,1,0:T(8,128)S(1)} custom-call(s32[1]{0:T(128)} %bitcast.column_ref.refs_0_, f32[4,520,128]{2,1,0:T(8,128)S(1)} %maps.1.refs_1_, f32[4,520,128]{2,1,0:T(8,128)S(1)} %shard_map.69.refs_2_, bf16[4,528,128]{2,1,0:T(8,128)(2,1)S(1)} %collective-permute-done.5.refs_3_), custom_call_target="tpu_custom_call" | custom-call | flops 15974400 | bytes 4194304 | tf_op jit(solution)/shard_map/pallas_call | solution.py:414
  66.5 32.6 %all_to_all.10 = f32[64,16,128]{2,1,0:T(8,128)S(1)} all-to-all(f32[64,16,128]{2,1,0:T(8,128)S(1)} %shard_map.70), channel_id=1, replica_groups=mesh['y'=8,'zl'=4,'c'=2,'zh'=2,'x'=4] {'y','zh','x'}, dimensions={0} | all-to-all | bytes 1048576 | tf_op jit(solution)/shard_map/all_to_all | solution.py:466
  99.1 0.1 reduce_sum.9
  99.1 0.6 slice_bitcast_fusion
  (4 shorter events, 0.0 us)
Async XLA Ops:
  0.6 6.6 %copy-start = (f32[1,64,128]{2,1,0:T(8,128)S(1)}, f32[1,64,128]{2,1,0:T(8,128)}, u32[]{:S(2)}) copy-start(f32[1,64,128]{2,1,0:T(8,128)} %param.5) | copy-start | bytes 98308
  0.6 6.8 %copy-start.1 = (f32[1,64,128]{2,1,0:T(8,128)S(1)}, f32[1,64,128]{2,1,0:T(8,128)}, u32[]{:S(2)}) copy-start(f32[1,64,128]{2,1,0:T(8,128)} %param.6) | copy-start | bytes 98308
  5.3 17.5 %collective-permute-start.2 = (bf16[4,2,528,128]{3,2,1,0:T(8,128)(2,1)}, bf16[4,2,528,128]{3,2,1,0:T(8,128)(2,1)S(1)}, u32[]{:S(2)}, u32[]{:S(2)}) collective-permute-start(bf16[4,2,528,128]{3,2,1,0:T(8,128)(2,1)} %get-tuple-element.11), channel_id=1, source_target_pairs={{0,8},{8,0},{1,9},{9,1},{2,10},{10,2},{3,11},{11,3},{4,12},{12,4},... | collective-permute-start | bytes 3244040 | tf_op jit(solution)/shard_map/ppermute | solution.py:449
  7.7 6.4 %collective-permute-start = (f32[3,64]{1,0:T(4,128)S(1)}, f32[3,64]{1,0:T(4,128)S(1)}, u32[]{:S(2)}, u32[]{:S(2)}) collective-permute-start(f32[3,64]{1,0:T(4,128)S(1)} %get-tuple-element.28), channel_id=1, source_target_pairs={{8,16},{16,8},{24,32},{32,24},{40,48},{48,40},{9,17},{17,9},{25,33... | collective-permute-start | bytes 2312 | tf_op jit(solution)/shard_map/ppermute | solution.py:439
  8.3 6.4 %collective-permute-start.1 = (f32[3,64]{1,0:T(4,128)S(1)}, f32[3,64]{1,0:T(4,128)S(1)}, u32[]{:S(2)}, u32[]{:S(2)}) collective-permute-start(f32[3,64]{1,0:T(4,128)S(1)} %get-tuple-element.29), channel_id=1, source_target_pairs={{0,8},{8,0},{1,9},{9,1},{2,10},{10,2},{3,11},{11,3},{4,12},{12,4},... | collective-permute-start | bytes 2312 | tf_op jit(solution)/shard_map/ppermute | solution.py:438
  15.7 25.9 %all-to-all-start = ((f32[8,136,128]{2,1,0:T(8,128)}), f32[8,136,128]{2,1,0:T(8,128)S(1)}, u32[]{:S(2)}, u32[]{:S(2)}) async-start(f32[8,136,128]{2,1,0:T(8,128)} %copies.1), calls=%async_computation | async-start | bytes 1114112 | tf_op jit(solution)/shard_map/all_to_all | solution.py:459
  24.7 21.9 %collective-permute-start.3 = (bf16[4,528,128]{2,1,0:T(8,128)(2,1)}, bf16[4,528,128]{2,1,0:T(8,128)(2,1)S(1)}, u32[]{:S(2)}, u32[]{:S(2)}) collective-permute-start(bf16[4,528,128]{2,1,0:T(8,128)(2,1)} %get-tuple-element.15), channel_id=1, source_target_pairs={{0,32},{4,36},{8,44},{12,40},{16,48},{20,52},{24,60},{28,56},{32,4... | collective-permute-start | bytes 1622024 | tf_op jit(solution)/shard_map/ppermute | solution.py:31
  30.8 28.3 %collective-permute-start.4 = (bf16[4,528,128]{2,1,0:T(8,128)(2,1)}, bf16[4,528,128]{2,1,0:T(8,128)(2,1)S(1)}, u32[]{:S(2)}, u32[]{:S(2)}) collective-permute-start(bf16[4,528,128]{2,1,0:T(8,128)(2,1)} %get-tuple-element.16), channel_id=1, source_target_pairs={{0,16},{4,20},{8,60},{12,56},{16,32},{20,36},{24,8},{28,12},{32,48... | collective-permute-start | bytes 1622024 | tf_op jit(solution)/shard_map/ppermute | solution.py:31
  32.9 29.4 %collective-permute-start.5 = (bf16[4,528,128]{2,1,0:T(8,128)(2,1)}, bf16[4,528,128]{2,1,0:T(8,128)(2,1)S(1)}, u32[]{:S(2)}, u32[]{:S(2)}) collective-permute-start(bf16[4,528,128]{2,1,0:T(8,128)(2,1)} %get-tuple-element.17), channel_id=1, source_target_pairs={{0,52},{4,48},{8,24},{12,28},{16,0},{20,4},{24,40},{28,44},{32,16}... | collective-permute-start | bytes 1622024 | tf_op jit(solution)/shard_map/ppermute | solution.py:31
